TPU v7x, 512 devices: a whole 4x4x16 slice. The times are simulated.
512 devices in a mesh: band: 64 (over x_lo, z, core), tile: 8 (over y, x_hi).
Axes of the slice: x: 4 (x_hi: 2, x_lo: 2; x = x_hi * 2 + x_lo), y: 4, z: 16, core: 2. Of those that a mesh axis runs over, the one named last changes fastest.
Arguments:
- alm: bfloat16 [1024, 9, 2, 1024], P('band', None, None, 'tile'), may hold values from -22 to 22
- legendre: bfloat16 [1024, 1024, 1024], P('band', 'tile'), may hold values from -0.1875 to 0.1875
- order_of_slot: int32 [1024], replicated, may hold values from 0 to 1023, each once
Outputs:
- ilc_map: float32 [1024, 4096], P('band', 'tile')
- ilc_alm: float32 [1024, 2, 1024], P('band', None, 'tile')
Inputs may be any that keep to these rules, and one draw needn't show every extreme that they name: `order_of_slot`: every order 0 to 1023 stands in exactly one slot.
All inputs are finite; a program needn't handle non-finite values.
Results may differ from a plain program's by a relative error of at most 0.02.
Values may be sent and summed in bfloat16 or wider, within the bound.
A program may use at most 64 MiB of HBM per device.

v0:
```python
import math

import jax
import jax.numpy as jnp
from jax import lax
from jax.sharding import PartitionSpec as P

C = 9
L = 1024
NLON = 4096
RB = 16
HALO = 32


RIDGE = 0.1
EPSILON = 1e-06


def sent_to_all(value, axis):
    copies = jnp.broadcast_to(value, (lax.axis_size(axis), *value.shape))
    return lax.all_to_all(copies, axis, split_axis=0, concat_axis=0, tiled=True)


def taken_together(value, axis):
    return sent_to_all(value, axis).astype(jnp.float32).sum(axis=0)


def with_halo(block, sides, width):
    for axis, dim in sides:
        count = lax.axis_size(axis)
        forward = [(i, i + 1) for i in range(count - 1)]
        forward.append((count - 1, 0))
        backward = [(target, source) for source, target in forward]
        low = lax.ppermute(
            lax.slice_in_dim(block, block.shape[dim] - width, None, axis=dim), axis, forward
        )
        high = lax.ppermute(lax.slice_in_dim(block, 0, width, axis=dim), axis, backward)
        block = jnp.concatenate([low, block, high], axis=dim)
    return block


def taken_together_2(value, axis):
    everything = sent_to_all(value, axis)
    return jnp.sum(everything, axis=0)


def make_basis(order_of_slot, begin_at, cell_count):
    columns = begin_at + jnp.arange(cell_count, dtype=jnp.int32)
    phases = order_of_slot[:, None] * columns[None, :] % NLON
    angles = phases.astype(jnp.float32) * (2.0 * math.pi / NLON)
    scaling = 1.0 / math.sqrt(L)
    return jnp.stack([jnp.cos(angles) * scaling, -jnp.sin(angles) * scaling]).astype(jnp.bfloat16)


def pair_table():
    return [(a_at, b_at) for a_at in range(C) for b_at in range(a_at, C)]


def window_sum(products):
    span_cells = products.shape[2]
    width_cells = span_cells - 2 * HALO
    total = products
    span = 1
    while span < 2 * HALO:
        total = total[:, :, :-span] + total[:, :, span:]
        span = span * 2
    return total[:, :, :width_cells] + products[:, :, 2 * HALO : 2 * HALO + width_cells]


def smooth_pairs(padded):
    widened = padded.astype(jnp.float32)
    products = jnp.stack([widened[a_at] * widened[b_at] for a_at, b_at in pair_table()])
    return window_sum(products) / (2 * HALO + 1)


def solve_weights(smoothed):
    entries = {}
    for pair_at, (a_at, b_at) in enumerate(pair_table()):
        entries[a_at, b_at] = smoothed[pair_at]
    trace_mean = entries[0, 0]
    for chan_at in range(1, C):
        trace_mean = trace_mean + entries[chan_at, chan_at]
    ridge_term = RIDGE * (trace_mean / C + EPSILON)
    factor = {}
    for row_at in range(C):
        for col_at in range(row_at + 1):
            running = entries[col_at, row_at]
            if row_at == col_at:
                running = running + ridge_term
            for inner_at in range(col_at):
                running = running - factor[row_at, inner_at] * factor[col_at, inner_at]
            if row_at == col_at:
                factor[row_at, row_at] = jnp.sqrt(running)
            else:
                factor[row_at, col_at] = running / factor[col_at, col_at]
    forward = []
    for row_at in range(C):
        running = jnp.ones_like(ridge_term)
        for inner_at in range(row_at):
            running = running - factor[row_at, inner_at] * forward[inner_at]
        forward.append(running / factor[row_at, row_at])
    backward = [forward[0]] * C
    for row_at in reversed(range(C)):
        running = forward[row_at]
        for inner_at in range(row_at + 1, C):
            running = running - factor[inner_at, row_at] * backward[inner_at]
        backward[row_at] = running / factor[row_at, row_at]
    normal = backward[0]
    for chan_at in range(1, C):
        normal = normal + backward[chan_at]
    return jnp.stack([solved / normal for solved in backward])


def to_band_layout(parts):
    return lax.all_to_all(parts, "band", split_axis=3, concat_axis=0, tiled=True)


def body(alm, legendre, order_of_slot):
    tile_count = lax.axis_size("tile")
    band_count = lax.axis_size("band")
    tile_at = lax.axis_index("tile")
    slot_count = alm.shape[0]
    lon_cells = NLON // tile_count
    partial_value = jnp.einsum("scel,slr->scer", alm, legendre, preferred_element_type=jnp.float32)
    own_basis = make_basis(order_of_slot, tile_at * lon_cells, lon_cells)
    shaped = partial_value.astype(jnp.bfloat16).reshape(slot_count, C, 2, band_count, RB)
    gathered = to_band_layout(shaped)
    summed = taken_together(gathered.astype(jnp.float32).astype(jnp.bfloat16), "tile").astype(
        jnp.float32
    )
    cycle_modes = summed.astype(jnp.bfloat16).reshape(L, C, 2, RB)
    channel_maps = jnp.einsum(
        "scer,esx->crx", cycle_modes, own_basis, preferred_element_type=jnp.float32
    ).astype(jnp.bfloat16)
    padded = with_halo(channel_maps, (("tile", 2),), HALO)
    weights = solve_weights(smooth_pairs(padded))
    ilc_map = jnp.sum(weights * channel_maps.astype(jnp.float32), axis=0)
    map_low = ilc_map.astype(jnp.bfloat16)
    cycle_partial = jnp.einsum(
        "rx,esx->res", map_low, own_basis, preferred_element_type=jnp.float32
    )
    routed = lax.all_to_all(cycle_partial, "band", split_axis=2, concat_axis=0, tiled=True)
    cycle_spectra = taken_together_2(routed, "tile").astype(jnp.bfloat16)
    ilc_alm = jnp.einsum(
        "slr,res->sel", legendre, cycle_spectra, preferred_element_type=jnp.float32
    )
    return (ilc_map, ilc_alm)


def solution(mesh):
    placed = (P("band", None, None, "tile"), P("band", "tile", None), P())
    return jax.shard_map(
        body,
        mesh=mesh,
        in_specs=placed,
        out_specs=(P("band", "tile"), P("band", None, "tile")),
        check_vma=False,
    )
```

profile of v0, /device:TPU:1, one launch (start us, length us, event | category | flops | bytes accessed | tf_op | source)
XLA Modules:
  0.0 249.8 jit_solution(7399007213763697263)
XLA Ops:
  0.6 2.9 %fusion.7 = bf16[16,9,2,1024]{3,1,2,0:T(8,128)(2,1)S(1)} fusion(bf16[16,128,1024]{2,1,0:T(8,128)(2,1)} %param.4, bf16[16,9,2,128]{3,2,1,0:T(2,128)(2,1)} %param.3), kind=kOutput, calls=%fused_computation.20 | convolution fusion | flops 75792384 | bytes 4857856 | tf_op jit(solution)/shard_map/scel,slr->scer/dot_general | solution.py:124
  3.5 4.9 %reshape.154 = bf16[16,9,2,64,16]{4,3,1,2,0:T(8,128)(2,1)} reshape(bf16[16,9,2,1024]{3,1,2,0:T(8,128)(2,1)S(1)} %fusion.7) | data formatting | bytes 1179648 | tf_op jit(solution)/shard_map/reshape | solution.py:126
  8.5 7.5 %copy.40 = bf16[16,9,2,64,16]{4,0,2,1,3:T(8,128)(2,1)} copy(bf16[16,9,2,64,16]{4,3,1,2,0:T(8,128)(2,1)} %reshape.154) | data formatting | bytes 1179648 | tf_op jit(solution)/shard_map/reshape | solution.py:126
  16.0 6.6 %reshape.155 = bf16[64,2,2304]{2,1,0:T(2,128)(2,1)S(1)} reshape(bf16[64,9,2,16,16]{4,3,2,1,0:T(8,128)(2,1)} %bitcast.50) | data formatting | bytes 1179648
  22.6 52.0 %all_to_all.46 = bf16[64,2,2304]{2,1,0:T(2,128)(2,1)S(1)} all-to-all(bf16[64,2,2304]{2,1,0:T(2,128)(2,1)S(1)} %reshape.155), channel_id=1, replica_groups=mesh['band'=64,'tile'=8] {'band'}, dimensions={0} | all-to-all | bytes 1179648 | tf_op jit(solution)/shard_map/all_to_all | solution.py:115
  74.7 4.7 %reshape.156 = bf16[64,9,2,16,16]{4,3,2,1,0:T(8,128)(2,1)} reshape(bf16[64,2,2304]{2,1,0:T(2,128)(2,1)S(1)} %all_to_all.46) | data formatting | bytes 1179648
  79.4 5.3 %bitcast_bitcast_fusion = bf16[64,16,9,2,1,16]{5,1,3,2,0,4:T(8,128)(2,1)} fusion(bf16[64,9,2,16,16]{4,3,2,1,0:T(8,128)(2,1)} %reshape.156), kind=kLoop, calls=%fused_computation.250 | loop fusion | bytes 1179648 | tf_op jit(solution)/shard_map/all_to_all | solution.py:115
  84.7 9.8 %copy.22 = bf16[64,16,9,2,1,16]{1,0,5,3,2,4:T(8,128)(2,1)} copy(bf16[64,16,9,2,1,16]{5,1,3,2,0,4:T(8,128)(2,1)} %bitcast_bitcast_fusion) | data formatting | bytes 1179648 | tf_op jit(solution)/shard_map/all_to_all | solution.py:115
  94.5 8.9 %all_to_all.35 = bf16[1024,9,2,16]{0,3,2,1:T(8,128)(2,1)S(1)} reshape(bf16[64,16,9,2,1,16]{1,0,5,3,2,4:T(8,128)(2,1)} %copy.22) | data formatting | bytes 1179648 | tf_op jit(solution)/shard_map/all_to_all | solution.py:115
  103.3 2.8 %broadcast_in_dim.8 = bf16[8,1024,9,2,1,16]{1,5,4,3,2,0:T(8,128)(2,1)} broadcast(bf16[1024,9,2,16]{0,3,2,1:T(8,128)(2,1)S(1)} %all_to_all.35), dimensions={1,2,3,5} | broadcast | bytes 5308416 | tf_op jit(solution)/shard_map/broadcast_in_dim | solution.py:20
  106.1 6.5 %all-to-all-start.1 = ((bf16[8,1024,9,2,1,16]{1,5,4,3,2,0:T(8,128)(2,1)}), bf16[8,1024,9,2,1,16]{1,5,4,3,2,0:T(8,128)(2,1)}, u32[]{:S(2)}, u32[]{:S(2)}) async-start(bf16[8,1024,9,2,1,16]{1,5,4,3,2,0:T(8,128)(2,1)} %broadcast_in_dim.8), calls=%async_computation.1 | async-start | bytes 9437184 | tf_op jit(solution)/shard_map/all_to_all | solution.py:21
  112.6 9.2 %multiply_convert_fusion.1 = (bf16[1,1024,512]{2,1,0:T(8,128)(2,1)S(1)}, bf16[1,1024,512]{2,1,0:T(8,128)(2,1)S(1)}) fusion(s32[512]{0:T(512)S(1)} %iota_add_fusion, s32[1024]{0:T(1024)S(1)} %copy-done.1), kind=kLoop, calls=%fused_computation.14 | loop fusion | flops 9961472 | bytes 2103296 | tf_op jit(solution)/shard_map/convert.1
  121.8 47.6 %all-to-all-done.1 = bf16[8,1024,9,2,1,16]{1,5,4,3,2,0:T(8,128)(2,1)} async-done(((bf16[8,1024,9,2,1,16]{1,5,4,3,2,0:T(8,128)(2,1)}), bf16[8,1024,9,2,1,16]{1,5,4,3,2,0:T(8,128)(2,1)}, u32[]{:S(2)}, u32[]{:S(2)}) %all-to-all-start.1) | async-done | bytes 4718624 | tf_op jit(solution)/shard_map/all_to_all | solution.py:21
  169.4 3.4 %reduce_sum.30 = bf16[1024,9,2,16]{0,3,2,1:T(8,128)(2,1)S(1)} reduce(bf16[8,1024,9,2,1,16]{1,5,4,3,2,0:T(8,128)(2,1)} %all-to-all-done.1, bf16[]{:T(256)} %constant.12.clone.1), dimensions={0,4}, to_apply=%region_0.1 | reduce | flops 2064384 | bytes 5308418 | tf_op jit(solution)/shard_map/reduce_sum | solution.py:25
  172.8 0.5 fusion.15
  173.3 0.1 fusion.121
  173.4 3.3 %collective-permute-start.1 = (bf16[9,16,32]{2,1,0:T(8,128)(2,1)S(1)}, bf16[9,16,32]{2,1,0:T(8,128)(2,1)S(1)}, u32[]{:S(2)}, u32[]{:S(2)}) collective-permute-start(bf16[9,16,32]{2,1,0:T(8,128)(2,1)S(1)} %get-tuple-element.14), channel_id=1, source_target_pairs={{1,0},{2,1},{3,2},{4,3},{5,4},{6,5},{7,6},{0,7},{9,8},{10,9},{11,1... | collective-permute-start | bytes 27656 | tf_op jit(solution)/shard_map/ppermute | solution.py:37
  176.7 3.7 %collective-permute-start = (bf16[9,16,32]{2,1,0:T(8,128)(2,1)S(1)}, bf16[9,16,32]{2,1,0:T(8,128)(2,1)S(1)}, u32[]{:S(2)}, u32[]{:S(2)}) collective-permute-start(bf16[9,16,32]{2,1,0:T(8,128)(2,1)S(1)} %get-tuple-element.13), channel_id=1, source_target_pairs={{0,1},{1,2},{2,3},{3,4},{4,5},{5,6},{6,7},{7,0},{8,9},{9,10},{10,1... | collective-permute-start | bytes 27656 | tf_op jit(solution)/shard_map/ppermute | solution.py:34
  180.4 4.6 %collective-permute-done = bf16[9,16,32]{2,1,0:T(8,128)(2,1)S(1)} collective-permute-done((bf16[9,16,32]{2,1,0:T(8,128)(2,1)S(1)}, bf16[9,16,32]{2,1,0:T(8,128)(2,1)S(1)}, u32[]{:S(2)}, u32[]{:S(2)}) %collective-permute-start) | collective-permute-done | bytes 9248 | tf_op jit(solution)/shard_map/ppermute | solution.py:34
  185.0 0.1 maximum_convert_fusion
  185.8 0.5 slice_add_fusion.4
  186.4 0.5 slice_add_fusion.3
  186.9 0.5 slice_add_fusion.2
  187.5 0.5 slice_add_fusion.1
  188.0 0.5 slice_add_fusion
  188.5 0.6 fusion.120
  189.1 0.5 fusion.10
  189.7 0.7 multiply_subtract_fusion
  190.4 0.6 constant_dynamic-update-slice_fusion.53
  191.0 0.6 constant_dynamic-update-slice_fusion.52
  191.7 0.6 constant_dynamic-update-slice_fusion.50
  192.3 0.6 constant_dynamic-update-slice_fusion.49
  192.9 0.6 constant_dynamic-update-slice_fusion.48
  193.5 0.6 constant_dynamic-update-slice_fusion.47
  194.1 0.6 constant_dynamic-update-slice_fusion.46
  194.6 0.6 constant_dynamic-update-slice_fusion.45
  195.3 0.6 fusion.11
  195.9 0.5 copy.23
  196.4 1.4 reshape.157
  197.9 24.3 %all_to_all.47 = f32[64,1,512]{2,1,0:T(1,128)S(1)} all-to-all(f32[64,1,512]{2,1,0:T(1,128)S(1)} %reshape.157), channel_id=1, replica_groups=mesh['band'=64,'tile'=8] {'band'}, dimensions={0} | all-to-all | bytes 262144 | tf_op jit(solution)/shard_map/all_to_all | solution.py:142
  222.2 0.5 broadcast.416
  222.7 0.9 reduce.2
  223.7 1.4 reshape.158
  225.1 0.6 copy.39
  225.7 0.6 all_to_all.40
  226.3 0.1 broadcast_in_dim.9
  226.4 19.3 %all_to_all.48 = f32[8,1024,2,16]{1,3,2,0:T(8,128)S(1)} all-to-all(f32[8,1024,2,16]{1,3,2,0:T(8,128)S(1)} %broadcast_in_dim.9), channel_id=1, replica_groups=mesh['band'=64,'tile'=8] {'tile'}, dimensions={0} | all-to-all | bytes 2097152 | tf_op jit(solution)/shard_map/all_to_all | solution.py:21
  245.8 4.0 %fusion.19 = f32[16,2,128]{2,1,0:T(2,128)} fusion(bf16[16,128,1024]{2,1,0:T(8,128)(2,1)} %param.4, bf16[1024,2,16]{0,2,1:T(8,128)(2,1)S(1)} %reduce_sum.32), kind=kOutput, calls=%fused_computation.85 | convolution fusion | flops 8388608 | bytes 4276224 | tf_op jit(solution)/shard_map/slr,res->sel/dot_general | solution.py:144
  (54 shorter events, 0.5 us)
Async XLA Ops:
  106.1 6.5 %copy-start.1 = (s32[1024]{0:T(1024)S(1)}, s32[1024]{0:T(1024)}, u32[]{:S(2)}) copy-start(s32[1024]{0:T(1024)} %param.5) | copy-start | bytes 12292
  106.1 63.3 %all-to-all-start.1 = ((bf16[8,1024,9,2,1,16]{1,5,4,3,2,0:T(8,128)(2,1)}), bf16[8,1024,9,2,1,16]{1,5,4,3,2,0:T(8,128)(2,1)}, u32[]{:S(2)}, u32[]{:S(2)}) async-start(bf16[8,1024,9,2,1,16]{1,5,4,3,2,0:T(8,128)(2,1)} %broadcast_in_dim.8), calls=%async_computation.1 | async-start | bytes 9437184 | tf_op jit(solution)/shard_map/all_to_all | solution.py:21
  173.4 7.0 %collective-permute-start.1 = (bf16[9,16,32]{2,1,0:T(8,128)(2,1)S(1)}, bf16[9,16,32]{2,1,0:T(8,128)(2,1)S(1)}, u32[]{:S(2)}, u32[]{:S(2)}) collective-permute-start(bf16[9,16,32]{2,1,0:T(8,128)(2,1)S(1)} %get-tuple-element.14), channel_id=1, source_target_pairs={{1,0},{2,1},{3,2},{4,3},{5,4},{6,5},{7,6},{0,7},{9,8},{10,9},{11,1... | collective-permute-start | bytes 27656 | tf_op jit(solution)/shard_map/ppermute | solution.py:37
  176.7 8.3 %collective-permute-start = (bf16[9,16,32]{2,1,0:T(8,128)(2,1)S(1)}, bf16[9,16,32]{2,1,0:T(8,128)(2,1)S(1)}, u32[]{:S(2)}, u32[]{:S(2)}) collective-permute-start(bf16[9,16,32]{2,1,0:T(8,128)(2,1)S(1)} %get-tuple-element.13), channel_id=1, source_target_pairs={{0,1},{1,2},{2,3},{3,4},{4,5},{5,6},{6,7},{7,0},{8,9},{9,10},{10,1... | collective-permute-start | bytes 27656 | tf_op jit(solution)/shard_map/ppermute | solution.py:34
  195.2 1.2 copy-start
where the time goes:
time: 251 us; the launch traced here: 250 us
  blocking collectives  95.7 us (38%)
  local copies, waits for them, and re-layouts  56.4 us (22%)
  waiting for transfers between devices  52.1 us (21%)
  other arithmetic  22.8 us (9%)
  starting transfers between devices  13.5 us (5%)
  matrix products  8.03 us (3%)
    all_to_all x1, blocking collectives, to_band_layout(): lax.all_to_all(parts, 'band', split_axis=3, concat_axis=0, tiled=True)  52 us
    all_to_all x1, waiting for transfers between devices, sent_to_all(): return lax.all_to_all(copies, axis, split_axis=0, concat_axis=0, tiled=True)  47.6 us
    all_to_all x1, blocking collectives, body(): lax.all_to_all(cycle_partial, 'band', split_axis=2, concat_axis=0, tiled=...  24.3 us
    all_to_all x3, local copies, waits for them, and re-layouts, to_band_layout(): lax.all_to_all(parts, 'band', split_axis=3, concat_axis=0, tiled=True)  23.9 us
    all_to_all x1, blocking collectives, sent_to_all(): return lax.all_to_all(copies, axis, split_axis=0, concat_axis=0, tiled=True)  19.3 us
    unnamed x8, local copies, waits for them, and re-layouts  14.2 us
    reshape x2, local copies, waits for them, and re-layouts, body(): partial_value.astype(jnp.bfloat16).reshape(slot_count, C, 2, band_count, RB)  12.5 us
    another operation x1, other arithmetic  9.19 us
  transfers between devices with their start and end apart: 3, of which 2 were waited for; matrix products, arithmetic and copies ran while one was open for 4% of the time, Pallas kernels for 0%

commit v1 on v0

v1 whole, which is shorter than its diff:
```python
import math

import jax
import jax.numpy as jnp
import numpy as np
from jax import lax
from jax.experimental import pallas as pl
from jax.experimental.pallas import tpu as pltpu
from jax.sharding import PartitionSpec as P

C = 9
HALO = 32
RIDGE = 0.1
EPSILON = 1e-06
NB = 64
NT = 8
F32 = jnp.float32
BF16 = jnp.bfloat16
MESH = pl.DeviceIdType.MESH


def tables():
    xl, j, xs = np.meshgrid(np.arange(8), np.arange(2), np.arange(4), indexing="ij")
    xa, jr = (xl + 8 * xs).reshape(-1), j.reshape(-1)
    m0, m1 = np.arange(128), np.arange(8)
    ang = 2 * np.pi * ((xa[:, None] * m1[None, :]) % 32) / 32
    same = (jr[:, None, None] == np.arange(2)[None, None, :]).astype(np.float64)
    cs, sn = np.cos(ang)[:, :, None] * same, np.sin(ang)[:, :, None] * same
    real = np.stack([cs, -sn], axis=3).reshape(64, 32)
    imag = np.stack([sn, cs], axis=3).reshape(64, 32)
    first = np.concatenate([real, imag], axis=0)
    high = first.astype(BF16).astype(np.float64)
    first = np.concatenate([high, first - high], axis=1)
    ang = 2 * np.pi * (xa[:, None] * m0[None, :]) / 4096
    twiddle = np.stack([np.cos(ang), np.sin(ang)])
    ang = 2 * np.pi * ((m0[:, None] * m0[None, :]) % 128) / 128
    second = np.concatenate([np.cos(ang), -np.sin(ang)], axis=0) / 32
    back = np.concatenate([np.cos(ang), -np.sin(ang)], axis=1) / 32
    ang = 2 * np.pi * ((m1[:, None] * xa[None, :]) % 32) / 32
    same = (np.arange(2)[:, None, None] == jr[None, None, :]).astype(np.float64)
    cs, sn = np.cos(ang)[None] * same, np.sin(ang)[None] * same
    e0 = np.concatenate([cs, sn], axis=2).reshape(16, 128)
    e1 = np.concatenate([-sn, cs], axis=2).reshape(16, 128)
    last = np.concatenate([e0, e1], axis=0)
    return (
        first.astype(BF16),
        twiddle.astype(np.float32),
        second.astype(BF16),
        back.astype(BF16),
        last.astype(BF16),
    )


def pair_table():
    return [(a, b) for a in range(C) for b in range(a, C)]


def window_sums(maps, smoothed):
    sub = lax.broadcasted_iota(jnp.int32, (8, 128), 0) % 4
    below = [jnp.where(sub >= k, 1.0, 0.0).astype(F32) for k in (1, 2, 3)]
    above = [jnp.where(sub <= 3 - k, 1.0, 0.0).astype(F32) for k in (1, 2, 3)]
    for at, (a, b) in enumerate(pair_table()):
        prod = [
            maps[a, 8 * i : 8 * i + 8, :] * maps[b, 8 * i : 8 * i + 8, :] for i in range(8)
        ]
        pre, post = [prod[0]], [prod[7]]
        for i in range(1, 8):
            pre.append(pre[-1] + prod[i])
            post.append(post[-1] + prod[7 - i])
        post = post[::-1]
        seg = pre[7]
        low = high = None
        for k in (1, 2, 3):
            down = below[k - 1] * pltpu.roll(seg, k, 0)
            up = above[k - 1] * pltpu.roll(seg, 8 - k, 0)
            low = down if low is None else low + down
            high = up if high is None else high + up
        total = seg + low + high
        for i in range(8):
            before = pltpu.roll(post[i] + high, 1, 1)
            after = pltpu.roll(pre[i] + low, 127, 1)
            smoothed[at, 8 * i : 8 * i + 8, :] = (before + total + after) * (
                1.0 / (2 * HALO + 1)
            )


def solve_cells(maps, smoothed, out):
    index = {}
    for at, (a, b) in enumerate(pair_table()):
        index[a, b] = at

    def step(i, _):
        rows = pl.ds(pl.multiple_of(i * 8, 8), 8)
        left = {key: smoothed[at, rows, :] for key, at in index.items()}
        trace = left[0, 0]
        for c in range(1, C):
            trace = trace + left[c, c]
        ridge = RIDGE * (trace * (1.0 / C) + EPSILON)
        for c in range(C):
            left[c, c] = left[c, c] + ridge
        ones = [jnp.ones((8, 128), F32) for _ in range(C)]
        vals = [maps[c, rows, :] for c in range(C)]
        top = bottom = None
        for k in range(C):
            inverse = 1.0 / left[k, k]
            scaled = ones[k] * inverse
            add_b, add_t = scaled * ones[k], scaled * vals[k]
            bottom = add_b if bottom is None else bottom + add_b
            top = add_t if top is None else top + add_t
            for r in range(k + 1, C):
                ratio = left[k, r] * inverse
                for q in range(r, C):
                    left[r, q] = left[r, q] - ratio * left[k, q]
                ones[r] = ones[r] - ratio * ones[k]
                vals[r] = vals[r] - ratio * vals[k]
        out[rows, :] = top / bottom
        return 0

    lax.fori_loop(0, 8, step, 0)


def turn(block):
    return jnp.transpose(block, (1, 0))


def kernel(
    alm_h, leg_h, ord_h, first_h, twid_h, second_h, back_h, last_h,
    map_o, alm_o,
    alm_v, leg_v, ord_v, first, twid, second, back, last,
    stage, parts, heard, slot_s, slot_r, turned, modes, gathered, to_order, to_slot,
    maps, smoothed, ilc, cells, cells_r, spec, spec_s, spec_r, spec_t, every,
    load_sem, send_sem, recv_sem,
):
    b = lax.axis_index("band")
    t = lax.axis_index("tile")
    owner_band = 8 * t + lax.div(b, 8)
    lane = lax.broadcasted_iota(jnp.int32, (8, 128), 1)

    loads = []
    for at, (src, dst) in enumerate(
        [(alm_h, alm_v)]
        + [(leg_h.at[pl.ds(4 * k, 4)], leg_v.at[pl.ds(4 * k, 4)]) for k in range(4)]
        + [(ord_h, ord_v), (first_h, first), (twid_h, twid), (second_h, second)]
        + [(back_h, back), (last_h, last)]
    ):
        copy = pltpu.make_async_copy(src, dst, load_sem.at[at])
        copy.start()
        loads.append(copy)

    bar = pltpu.get_barrier_semaphore()

    def greet_band(d, _):
        pl.semaphore_signal(
            bar, inc=1, device_id={"band": lax.rem(b + d, NB), "tile": t}, device_id_type=MESH
        )
        return 0

    lax.fori_loop(1, NB, greet_band, 0)
    for d in range(1, NT):
        pl.semaphore_signal(
            bar, inc=1, device_id={"band": b, "tile": lax.rem(t + d, NT)}, device_id_type=MESH
        )
    source_tile = lax.div(b, 8)
    for k in range(8):
        source_band = 8 * lax.rem(b, 8) + k
        own = jnp.logical_and(source_band == b, source_tile == t)

        @pl.when(jnp.logical_not(own))
        def _():
            pl.semaphore_signal(
                bar, inc=1, device_id={"band": source_band, "tile": source_tile},
                device_id_type=MESH,
            )

    loads[0].wait()
    for k in range(4):
        loads[1 + k].wait()
        for s in range(4 * k, 4 * k + 4):
            left = alm_v[s].reshape(18, 128)
            out = jnp.dot(left, leg_v[s], preferred_element_type=F32)
            for q in range(NT):
                stage[q, pl.ds(s, 18, stride=16), :] = out[:, 128 * q : 128 * q + 128]
    for q in range(NT):
        parts[q] = stage[q].astype(BF16)

    pl.semaphore_wait(bar, 78 - jnp.where(owner_band == b, 1, 0))

    for d in range(1, NT):
        other = lax.rem(t + d, NT)
        pltpu.make_async_remote_copy(
            src_ref=parts.at[other], dst_ref=heard.at[t], send_sem=send_sem.at[0],
            recv_sem=recv_sem.at[0], device_id={"band": b, "tile": other}, device_id_type=MESH,
        ).start()
    pltpu.make_async_copy(parts.at[t], heard.at[t], recv_sem.at[0]).start()

    for copy in loads[5:]:
        copy.wait()
    orders = ord_v[...].astype(F32)
    cols = turn(jnp.concatenate([orders, jnp.zeros((120, 128), F32)], axis=0))
    turned[0:128, :] = cols
    wide = lax.broadcasted_iota(jnp.int32, (8, 1024), 1).astype(F32)
    for s in range(16):
        pick = turned[pl.ds(s, 8, stride=16), :]
        for h in range(0, 8, 2):
            rows = [
                jnp.where(pick[:, k : k + 1] == wide, 1.0, 0.0) for k in (h, h + 1)
            ]
            to_order[s * 64 + h * 8 : s * 64 + h * 8 + 16, :] = jnp.concatenate(
                rows, axis=0
            ).astype(BF16)
    tall = lax.broadcasted_iota(jnp.int32, (128, 128), 0).astype(F32)
    for h in range(8):
        row = jnp.broadcast_to(orders[h : h + 1, :], (128, 128))
        for k in range(8):
            to_slot[128 * k : 128 * k + 128, 128 * h : 128 * h + 128] = jnp.where(
                row == tall + 128.0 * k, 1.0, 0.0
            ).astype(BF16)

    pltpu.make_async_copy(heard, heard, recv_sem.at[0]).wait()
    total = heard[0].astype(F32)
    for q in range(1, NT):
        total = total + heard[q].astype(F32)
    total = jnp.concatenate([total, jnp.zeros((96, 128), F32)], axis=0)
    for k in range(3):
        block = turn(total[128 * k : 128 * k + 128])
        slot_s[:, k] = block.astype(BF16).reshape(NB, 2, 128)

    def send_slots(d, _):
        other = lax.rem(b + d, NB)
        pltpu.make_async_remote_copy(
            src_ref=slot_s.at[other], dst_ref=slot_r.at[b], send_sem=send_sem.at[1],
            recv_sem=recv_sem.at[1], device_id={"band": other, "tile": t}, device_id_type=MESH,
        ).start()
        return 0

    lax.fori_loop(1, NB, send_slots, 0)
    pltpu.make_async_copy(slot_s.at[b], slot_r.at[b], recv_sem.at[1]).start()
    pltpu.make_async_copy(slot_r, slot_r, recv_sem.at[1]).wait()

    for k in range(3):
        block = slot_r[:, k].astype(F32)
        block = jnp.concatenate([block[:, 0, :], block[:, 1, :]], axis=0)
        turned[128 * k : 128 * k + 128, :] = turn(block)
    lane24 = lax.broadcasted_iota(jnp.int32, (24, 128), 1)
    pieces = []
    for p in range(8):
        even = turned[pl.ds(2 * p, 24, stride=16), :]
        odd = turned[pl.ds(2 * p + 1, 24, stride=16), :]
        first_r = jnp.where(lane24 < 64, even, pltpu.roll(odd, 64, 1))
        second_r = jnp.where(lane24 < 64, pltpu.roll(even, 64, 1), odd)
        pieces.append(jnp.concatenate([first_r, second_r], axis=0).astype(BF16))
    ordered = jnp.dot(
        jnp.concatenate(pieces, axis=1), to_order[...], preferred_element_type=F32
    )
    for k in range(8):
        modes[k] = ordered[:, 128 * k : 128 * k + 128]
    for c in range(C):
        for k in range(8):
            gathered[c, 4 * k : 4 * k + 2, :] = modes[k, 2 * c : 2 * c + 2, :]
            gathered[c, 4 * k + 2 : 4 * k + 4, :] = modes[k, 24 + 2 * c : 26 + 2 * c, :]

    twr, twi = twid[0], twid[1]
    for c in range(C):
        data = gathered[c].astype(BF16)
        grid = jnp.dot(
            first[...], jnp.concatenate([data, data], axis=0), preferred_element_type=F32
        )
        re, im = grid[:64], grid[64:]
        both = jnp.concatenate([re * twr - im * twi, re * twi + im * twr], axis=1)
        maps[c] = (
            jnp.dot(both.astype(BF16), second[...], preferred_element_type=F32)
            .astype(BF16)
            .astype(F32)
        )

    window_sums(maps, smoothed)
    solve_cells(maps, smoothed, ilc)

    grid = jnp.dot(ilc[...].astype(BF16), back[...], preferred_element_type=F32)
    re, im = grid[:, :128], grid[:, 128:]
    both = jnp.concatenate([re * twr + im * twi, im * twr - re * twi], axis=0)
    spec[...] = jnp.dot(last[...], both.astype(BF16), preferred_element_type=F32)
    flat = jnp.concatenate([spec[pl.ds(k, 4, stride=8), :] for k in range(8)], axis=1)
    flat = jnp.concatenate([flat, jnp.zeros((4, 1024), F32)], axis=0)
    placed = jnp.dot(flat.astype(BF16), to_slot[...], preferred_element_type=F32)
    for k in range(8):
        spec_s[k] = placed[0:4, 128 * k : 128 * k + 128].astype(BF16)

    def send_spectra(d, _):
        other = lax.rem(b + d, NB)
        pltpu.make_async_remote_copy(
            src_ref=spec_s.at[lax.div(other, 8)], dst_ref=spec_r.at[b], send_sem=send_sem.at[2],
            recv_sem=recv_sem.at[2], device_id={"band": other, "tile": t}, device_id_type=MESH,
        ).start()
        return 0

    lax.fori_loop(1, NB, send_spectra, 0)
    pltpu.make_async_copy(spec_s.at[lax.div(b, 8)], spec_r.at[b], recv_sem.at[2]).start()

    lines = jnp.concatenate(
        [ilc[pl.ds(k, 8, stride=8), :] for k in range(8)] + [jnp.zeros((64, 128), F32)], axis=0
    )
    turned[0:128, :] = turn(lines)
    lane32 = lax.broadcasted_iota(jnp.int32, (32, 128), 1)
    for j in range(2):
        line = None
        for k in range(4):
            part = turned[pl.ds(k, 32, stride=4), :]
            part = pltpu.roll(part, (32 * k - 32 * j) % 128, 1) if k != j else part
            keep = jnp.logical_and(lane32 >= 32 * k, lane32 < 32 * k + 32)
            part = jnp.where(keep, part, 0.0)
            line = part if line is None else line + part
        cells[pl.ds(j, 32, stride=2), :] = line
    place = pl.ds(pl.multiple_of(8 * lax.rem(b, 8), 8), 8)
    for q in range(NT):
        own = jnp.logical_and(owner_band == b, t == q)

        @pl.when(own)
        def _():
            pltpu.make_async_copy(
                cells.at[8 * q : 8 * q + 8], cells_r.at[place], recv_sem.at[4]
            ).start()

        @pl.when(jnp.logical_not(own))
        def _():
            pltpu.make_async_remote_copy(
                src_ref=cells.at[8 * q : 8 * q + 8], dst_ref=cells_r.at[place],
                send_sem=send_sem.at[4], recv_sem=recv_sem.at[4],
                device_id={"band": owner_band, "tile": q}, device_id_type=MESH,
            ).start()

    pltpu.make_async_copy(spec_r, spec_r, recv_sem.at[2]).wait()
    start = pl.multiple_of(16 * lax.rem(b, 8), 16)
    block = spec_r[...].astype(F32)
    for e in range(2):
        spec_t[e] = turn(block[:, 2 * e : 2 * e + 2, :].reshape(128, 128))
    own_s = [spec_t[e, pl.ds(start, 16), :] for e in range(2)]
    every[t] = jnp.concatenate(own_s, axis=0).astype(BF16)
    for d in range(1, NT):
        other = lax.rem(t + d, NT)
        pltpu.make_async_remote_copy(
            src_ref=every.at[t], dst_ref=every.at[t], send_sem=send_sem.at[3],
            recv_sem=recv_sem.at[3], device_id={"band": b, "tile": other}, device_id_type=MESH,
        ).start()
    seven = every.at[pl.ds(0, NT - 1)]
    pltpu.make_async_copy(seven, seven, recv_sem.at[3]).wait()
    full = jnp.concatenate([every[q] for q in range(NT)], axis=1)
    for s in range(16):
        out = lax.dot_general(
            full, leg_v[s], (((1,), (1,)), ((), ())), preferred_element_type=F32
        )
        alm_o[s, 0:1, :] = out[s : s + 1]
        alm_o[s, 1:2, :] = out[16 + s : 17 + s]

    pltpu.make_async_copy(cells_r, cells_r, recv_sem.at[4]).wait()
    for q in range(4):
        for j in range(2):
            ilc[pl.ds(16 * q + j, 8, stride=2), :] = cells_r[pl.ds(2 * q + j, 8, stride=8), :]
        map_o[:, 128 * q : 128 * q + 128] = ilc[16 * q : 16 * q + 16, :]

    sent = parts.at[pl.ds(0, NT - 1)]
    pltpu.make_async_copy(sent, sent, send_sem.at[0]).wait()
    sent = slot_s.at[pl.ds(0, NB - 1)]
    pltpu.make_async_copy(sent, sent, send_sem.at[1]).wait()
    sent = spec_r.at[pl.ds(0, NB - 1)]
    pltpu.make_async_copy(sent, sent, send_sem.at[2]).wait()
    pltpu.make_async_copy(seven, seven, send_sem.at[3]).wait()
    mine = owner_band == b

    @pl.when(mine)
    def _():
        sent = cells.at[0:56]
        pltpu.make_async_copy(sent, sent, send_sem.at[4]).wait()

    @pl.when(jnp.logical_not(mine))
    def _():
        pltpu.make_async_copy(cells, cells, send_sem.at[4]).wait()


def body(alm, legendre, order_of_slot):
    any_space = pl.BlockSpec(memory_space=pl.ANY)
    vmem = pl.BlockSpec(memory_space=pltpu.VMEM)
    first, twid, second, back, last = tables()
    scratch = [
        ((16, C, 2, 128), BF16),
        ((16, 128, 1024), BF16),
        ((8, 128), jnp.int32),
        (first.shape, BF16),
        (twid.shape, F32),
        (second.shape, BF16),
        (back.shape, BF16),
        (last.shape, BF16),
        ((NT, 288, 128), F32),
        ((NT, 288, 128), BF16),
        ((NT, 288, 128), BF16),
        ((NB, 3, 2, 128), BF16),
        ((NB, 3, 2, 128), BF16),
        ((384, 128), F32),
        ((8, 48, 128), F32),
        ((C, 32, 128), F32),
        ((1024, 1024), BF16),
        ((1024, 1024), BF16),
        ((C, 64, 128), F32),
        ((45, 64, 128), F32),
        ((64, 128), F32),
        ((64, 128), F32),
        ((64, 128), F32),
        ((32, 128), F32),
        ((8, 4, 128), BF16),
        ((NB, 4, 128), BF16),
        ((2, 128, 128), F32),
        ((NT, 32, 128), BF16),
    ]
    return pl.pallas_call(
        kernel,
        out_shape=(
            jax.ShapeDtypeStruct((16, 512), F32),
            jax.ShapeDtypeStruct((16, 2, 128), F32),
        ),
        in_specs=[any_space] * 8,
        out_specs=(vmem, vmem),
        scratch_shapes=[pltpu.VMEM(shape, kind) for shape, kind in scratch]
        + [
            pltpu.SemaphoreType.DMA((11,)),
            pltpu.SemaphoreType.DMA((5,)),
            pltpu.SemaphoreType.DMA((5,)),
        ],
        compiler_params=pltpu.CompilerParams(
            collective_id=0, has_side_effects=True, vmem_limit_bytes=48 * 1024 * 1024
        ),
    )(alm, legendre, order_of_slot.reshape(8, 128), first, twid, second, back, last)


def solution(mesh):
    placed = (P("band", None, None, "tile"), P("band", "tile", None), P())
    return jax.shard_map(
        body,
        mesh=mesh,
        in_specs=placed,
        out_specs=(P("band", "tile"), P("band", None, "tile")),
        check_vma=False,
    )
```

time: 251 us -> 72.5 us (0.29)
  blocking collectives: 95.7 us -> 0 us
  Pallas kernels: 0 us -> 62.4 us
  waiting for transfers between devices: 52.1 us -> 0 us
  local copies, waits for them, and re-layouts: 56.4 us -> 8.94 us
  other arithmetic: 22.8 us -> 0 us
  starting transfers between devices: 13.5 us -> 0 us
  matrix products: 8.03 us -> 0 us
    all_to_all x3 -> x0, blocking collectives: 95.7 us -> none  [the longest x1 52 us: to_band_layout(): lax.all_to_all(parts, 'band', split_axis=3, concat_axis=0, tiled=True)]
    pallas_call x0 -> x1, Pallas kernels: none -> 62.4 us  [body(): pl.pallas_call(kernel, out_shape=(jax.ShapeDtypeStruct((16, 512), F32), j...]
    all_to_all x1 -> x0, waiting for transfers between devices: 47.6 us -> none  [sent_to_all(): return lax.all_to_all(copies, axis, split_axis=0, concat_axis=0, tiled=True)]
    all_to_all x6 -> x0, local copies, waits for them, and re-layouts: 25.7 us -> none  [the longest x3 23.9 us: to_band_layout(): lax.all_to_all(parts, 'band', split_axis=3, concat_axis=0, tiled=True)]
    reshape x2 -> x0, local copies, waits for them, and re-layouts: 12.5 us -> none  [body(): partial_value.astype(jnp.bfloat16).reshape(slot_count, C, 2, band_count, RB)]
    another operation x3 -> x0, other arithmetic: 9.75 us -> none
    dot_general x4 -> x0, matrix products: 8.03 us -> none  [the longest x1 3.99 us: body(): jnp.einsum('slr,res->sel', legendre, cycle_spectra, preferred_element_typ...]
    ppermute x2 -> x0, starting transfers between devices: 7.01 us -> none  [the longest x1 3.74 us: with_halo(): lax.ppermute(lax.slice_in_dim(block, block.shape[dim] - width, None, axis...]
  transfers between devices with their start and end apart: 3 -> 0, of which waited for: 2 -> 0; matrix products, arithmetic and copies ran while one was open for 4% -> 0% of each run, Pallas kernels for 0% -> 0%
where the time goes in v1:
time: 72.5 us; the launch traced here: 72 us
  Pallas kernels  62.4 us (86%)
  local copies, waits for them, and re-layouts  8.94 us (12%)
    pallas_call x1, Pallas kernels, body(): pl.pallas_call(kernel, out_shape=(jax.ShapeDtypeStruct((16, 512), F32), j...  62.4 us
    unnamed x18, local copies, waits for them, and re-layouts  8.94 us

profile of v1, /device:TPU:1, one launch (start us, length us, event | category | flops | bytes accessed | tf_op | source)
XLA Modules:
  0.0 72.0 jit_solution(602309243332749588)
XLA Ops:
  0.6 0.0 copy-start
  0.6 2.2 %copy-done = bf16[16,128,1024]{2,1,0:T(8,128)(2,1)S(1)} copy-done((bf16[16,128,1024]{2,1,0:T(8,128)(2,1)S(1)}, bf16[16,128,1024]{2,1,0:T(8,128)(2,1)}, u32[]{:S(2)}) %copy-start) | copy-done | bytes 4194328
  2.8 0.0 copy-start.1
  2.8 0.9 %copy-done.1 = bf16[16,9,2,128]{3,2,1,0:T(2,128)(2,1)S(1)} copy-done((bf16[16,9,2,128]{3,2,1,0:T(2,128)(2,1)S(1)}, bf16[16,9,2,128]{3,2,1,0:T(2,128)(2,1)}, u32[]{:S(2)}) %copy-start.1) | copy-done | bytes 73752
  3.7 0.0 copy-start.2
  3.7 0.8 %copy-done.2 = bf16[128,256]{1,0:T(8,128)(2,1)S(1)} copy-done((bf16[128,256]{1,0:T(8,128)(2,1)S(1)}, bf16[128,256]{1,0:T(8,128)(2,1)}, u32[]{:S(2)}) %copy-start.2) | copy-done | bytes 65560
  4.5 0.0 copy-start.3
  4.5 0.8 %copy-done.3 = bf16[256,128]{1,0:T(8,128)(2,1)S(1)} copy-done((bf16[256,128]{1,0:T(8,128)(2,1)S(1)}, bf16[256,128]{1,0:T(8,128)(2,1)}, u32[]{:S(2)}) %copy-start.3) | copy-done | bytes 65560
  5.4 0.0 copy-start.4
  5.4 0.8 %copy-done.4 = f32[2,64,128]{2,1,0:T(8,128)S(1)} copy-done((f32[2,64,128]{2,1,0:T(8,128)S(1)}, f32[2,64,128]{2,1,0:T(8,128)}, u32[]{:S(2)}) %copy-start.4) | copy-done | bytes 65560
  6.2 0.0 copy-start.5
  6.2 0.8 %copy-done.5 = bf16[128,64]{1,0:T(8,128)(2,1)S(1)} copy-done((bf16[128,64]{1,0:T(8,128)(2,1)S(1)}, bf16[128,64]{1,0:T(8,128)(2,1)}, u32[]{:S(2)}) %copy-start.5) | copy-done | bytes 16408
  7.0 0.0 copy-start.6
  7.0 0.7 copy-done.6
  7.7 0.0 copy-start.7
  7.7 0.7 copy-done.7
  8.4 62.4 %shard_map.95 = (f32[16,512]{1,0:T(8,128)S(1)}, f32[16,2,128]{2,1,0:T(2,128)S(1)}) custom-call(bf16[16,9,2,128]{3,2,1,0:T(2,128)(2,1)S(1)} %copy-done.1, bf16[16,128,1024]{2,1,0:T(8,128)(2,1)S(1)} %copy-done, s32[8,128]{1,0:T(8,128)S(1)} %bitcast.1, bf16[128,64]{1,0:T(8,128)(2,1)S(1)} %copy-done.5, f32[2,64,128]{2,1,0:T(8,128)S(1)} %copy-done.4, ...), custom_call_target="tpu_custom_call" | custom-call | tf_op jit(solution)/shard_map/pallas_call | solution.py:414
  70.8 0.6 copy.12
  71.4 0.6 copy.13
Async XLA Ops:
  0.6 2.2 %copy-start = (bf16[16,128,1024]{2,1,0:T(8,128)(2,1)S(1)}, bf16[16,128,1024]{2,1,0:T(8,128)(2,1)}, u32[]{:S(2)}) copy-start(bf16[16,128,1024]{2,1,0:T(8,128)(2,1)} %leg_h.1) | copy-start | bytes 12582916
  2.8 0.9 %copy-start.1 = (bf16[16,9,2,128]{3,2,1,0:T(2,128)(2,1)S(1)}, bf16[16,9,2,128]{3,2,1,0:T(2,128)(2,1)}, u32[]{:S(2)}) copy-start(bf16[16,9,2,128]{3,2,1,0:T(2,128)(2,1)} %alm_h.1) | copy-start | bytes 221188
  3.7 0.8 %copy-start.2 = (bf16[128,256]{1,0:T(8,128)(2,1)S(1)}, bf16[128,256]{1,0:T(8,128)(2,1)}, u32[]{:S(2)}) copy-start(bf16[128,256]{1,0:T(8,128)(2,1)} %constant.13.clone.back_h) | copy-start | bytes 196612
  4.5 0.8 %copy-start.3 = (bf16[256,128]{1,0:T(8,128)(2,1)S(1)}, bf16[256,128]{1,0:T(8,128)(2,1)}, u32[]{:S(2)}) copy-start(bf16[256,128]{1,0:T(8,128)(2,1)} %constant.12.clone.second_h) | copy-start | bytes 196612
  5.4 0.8 %copy-start.4 = (f32[2,64,128]{2,1,0:T(8,128)S(1)}, f32[2,64,128]{2,1,0:T(8,128)}, u32[]{:S(2)}) copy-start(f32[2,64,128]{2,1,0:T(8,128)} %constant.11.clone.twid_h) | copy-start | bytes 196612
  6.2 0.8 %copy-start.5 = (bf16[128,64]{1,0:T(8,128)(2,1)S(1)}, bf16[128,64]{1,0:T(8,128)(2,1)}, u32[]{:S(2)}) copy-start(bf16[128,64]{1,0:T(8,128)(2,1)} %constant.10.clone.first_h) | copy-start | bytes 49156
  7.0 0.7 copy-start.6
  7.7 0.7 copy-start.7

commit v2 on v1

--- a/solution.py
+++ b/solution.py
@@ -17,6 +17,43 @@
 F32 = jnp.float32
 BF16 = jnp.bfloat16
 MESH = pl.DeviceIdType.MESH
+
+
+SCRATCH = {
+    "alm_v": ((16, C, 2, 128), BF16),
+    "leg_v": ((16, 128, 1024), BF16),
+    "ord_v": ((8, 128), jnp.int32),
+    "first": ((128, 64), BF16),
+    "twid": ((2, 64, 128), F32),
+    "second": ((256, 128), BF16),
+    "back": ((128, 256), BF16),
+    "last": ((128, 128), BF16),
+    "stage": ((NT, 288, 128), F32),
+    "parts": ((NT, 288, 128), BF16),
+    "heard": ((NT, 288, 128), BF16),
+    "slot_s": ((NB, 3, 2, 128), BF16),
+    "slot_r": ((NB, 3, 2, 128), BF16),
+    "turned": ((384, 128), F32),
+    "modes": ((8, 48, 128), F32),
+    "gathered": ((C, 32, 128), F32),
+    "to_order": ((1024, 1024), BF16),
+    "to_slot": ((1024, 1024), BF16),
+    "maps": ((C, 64, 128), F32),
+    "smoothed": ((45, 64, 128), F32),
+    "ilc": ((64, 128), F32),
+    "cells": ((64, 128), F32),
+    "cells_r": ((64, 128), F32),
+    "spec": ((128, 128), F32),
+    "spec_s": ((16, 2, 128), BF16),
+    "spec_r": ((NB, 2, 128), BF16),
+    "spec_t": ((128, 128), F32),
+    "every": ((NT, 32, 128), BF16),
+    "sums": ((16, 32, 128), F32),
+}
+
+
+def scratch_list():
+    return [pltpu.VMEM(shape, kind) for shape, kind in SCRATCH.values()]
 
 
 def tables():
@@ -41,7 +78,8 @@
     cs, sn = np.cos(ang)[None] * same, np.sin(ang)[None] * same
     e0 = np.concatenate([cs, sn], axis=2).reshape(16, 128)
     e1 = np.concatenate([-sn, cs], axis=2).reshape(16, 128)
-    last = np.concatenate([e0, e1], axis=0)
+    none = np.zeros((48, 128))
+    last = np.concatenate([e0, none, e1, none], axis=0)
     return (
         first.astype(BF16),
         twiddle.astype(np.float32),
@@ -119,6 +157,22 @@
     lax.fori_loop(0, 8, step, 0)
 
 
+def band_peer(d, b):
+    k, i = lax.div(d, 4), lax.rem(d, 4)
+    dz = lax.rem(24 + (1 - 2 * lax.rem(k, 2)) * lax.div(k + 1, 2), 16)
+    x = lax.rem(lax.div(b, 32) + lax.div(i, 2) + 1, 2)
+    z = lax.rem(lax.rem(lax.div(b, 2), 16) + dz, 16)
+    core = lax.rem(lax.rem(b, 2) + lax.rem(i, 2) + 1, 2)
+    return (x * 16 + z) * 2 + core
+
+
+FAR_FIRST = ((2, 1), (1, 1), (3, 1), (2, 0), (0, 1), (1, 0), (3, 0))
+
+
+def tile_peer(t, dy, dx):
+    return 2 * lax.rem(lax.div(t, 2) + dy, 4) + lax.rem(lax.rem(t, 2) + dx, 2)
+
+
 def turn(block):
     return jnp.transpose(block, (1, 0))
 
@@ -128,8 +182,8 @@
     map_o, alm_o,
     alm_v, leg_v, ord_v, first, twid, second, back, last,
     stage, parts, heard, slot_s, slot_r, turned, modes, gathered, to_order, to_slot,
-    maps, smoothed, ilc, cells, cells_r, spec, spec_s, spec_r, spec_t, every,
-    load_sem, send_sem, recv_sem,
+    maps, smoothed, ilc, cells, cells_r, spec, spec_s, spec_r, spec_t, every, sums,
+    load_sem, send_sem, recv_sem, tile_sem,
 ):
     b = lax.axis_index("band")
     t = lax.axis_index("tile")
@@ -151,26 +205,15 @@
 
     def greet_band(d, _):
         pl.semaphore_signal(
-            bar, inc=1, device_id={"band": lax.rem(b + d, NB), "tile": t}, device_id_type=MESH
+            bar, inc=1, device_id={"band": band_peer(d, b), "tile": t}, device_id_type=MESH
         )
         return 0
 
-    lax.fori_loop(1, NB, greet_band, 0)
+    lax.fori_loop(0, NB - 1, greet_band, 0)
     for d in range(1, NT):
         pl.semaphore_signal(
             bar, inc=1, device_id={"band": b, "tile": lax.rem(t + d, NT)}, device_id_type=MESH
         )
-    source_tile = lax.div(b, 8)
-    for k in range(8):
-        source_band = 8 * lax.rem(b, 8) + k
-        own = jnp.logical_and(source_band == b, source_tile == t)
-
-        @pl.when(jnp.logical_not(own))
-        def _():
-            pl.semaphore_signal(
-                bar, inc=1, device_id={"band": source_band, "tile": source_tile},
-                device_id_type=MESH,
-            )
 
     loads[0].wait()
     for k in range(4):
@@ -183,10 +226,10 @@
     for q in range(NT):
         parts[q] = stage[q].astype(BF16)
 
-    pl.semaphore_wait(bar, 78 - jnp.where(owner_band == b, 1, 0))
-
-    for d in range(1, NT):
-        other = lax.rem(t + d, NT)
+    pl.semaphore_wait(bar, 70)
+
+    for dy, dx in FAR_FIRST:
+        other = tile_peer(t, dy, dx)
         pltpu.make_async_remote_copy(
             src_ref=parts.at[other], dst_ref=heard.at[t], send_sem=send_sem.at[0],
             recv_sem=recv_sem.at[0], device_id={"band": b, "tile": other}, device_id_type=MESH,
@@ -226,14 +269,14 @@
         slot_s[:, k] = block.astype(BF16).reshape(NB, 2, 128)
 
     def send_slots(d, _):
-        other = lax.rem(b + d, NB)
+        other = band_peer(d, b)
         pltpu.make_async_remote_copy(
             src_ref=slot_s.at[other], dst_ref=slot_r.at[b], send_sem=send_sem.at[1],
             recv_sem=recv_sem.at[1], device_id={"band": other, "tile": t}, device_id_type=MESH,
         ).start()
         return 0
 
-    lax.fori_loop(1, NB, send_slots, 0)
+    lax.fori_loop(0, NB - 1, send_slots, 0)
     pltpu.make_async_copy(slot_s.at[b], slot_r.at[b], recv_sem.at[1]).start()
     pltpu.make_async_copy(slot_r, slot_r, recv_sem.at[1]).wait()
 
@@ -276,26 +319,30 @@
     window_sums(maps, smoothed)
     solve_cells(maps, smoothed, ilc)
 
+    twr, twi = twid[0], twid[1]
     grid = jnp.dot(ilc[...].astype(BF16), back[...], preferred_element_type=F32)
     re, im = grid[:, :128], grid[:, 128:]
     both = jnp.concatenate([re * twr + im * twi, im * twr - re * twi], axis=0)
     spec[...] = jnp.dot(last[...], both.astype(BF16), preferred_element_type=F32)
-    flat = jnp.concatenate([spec[pl.ds(k, 4, stride=8), :] for k in range(8)], axis=1)
-    flat = jnp.concatenate([flat, jnp.zeros((4, 1024), F32)], axis=0)
+    flat = jnp.concatenate([spec[pl.ds(k, 16, stride=8), :] for k in range(8)], axis=1)
     placed = jnp.dot(flat.astype(BF16), to_slot[...], preferred_element_type=F32)
+    half = lax.broadcasted_iota(jnp.int32, (8, 128), 1) < 64
     for k in range(8):
-        spec_s[k] = placed[0:4, 128 * k : 128 * k + 128].astype(BF16)
-
+        e0, e1 = (placed[8 * e : 8 * e + 8, 128 * k : 128 * k + 128] for e in range(2))
+        low = jnp.where(half, e0, pltpu.roll(e1, 64, 1))
+        high = jnp.where(half, pltpu.roll(e0, 64, 1), e1)
+        spec_s[2 * k] = low[0:2].astype(BF16)
+        spec_s[2 * k + 1] = high[0:2].astype(BF16)
     def send_spectra(d, _):
-        other = lax.rem(b + d, NB)
+        other = band_peer(d, b)
         pltpu.make_async_remote_copy(
-            src_ref=spec_s.at[lax.div(other, 8)], dst_ref=spec_r.at[b], send_sem=send_sem.at[2],
+            src_ref=spec_s.at[lax.div(other, 4)], dst_ref=spec_r.at[b], send_sem=send_sem.at[2],
             recv_sem=recv_sem.at[2], device_id={"band": other, "tile": t}, device_id_type=MESH,
         ).start()
         return 0
 
-    lax.fori_loop(1, NB, send_spectra, 0)
-    pltpu.make_async_copy(spec_s.at[lax.div(b, 8)], spec_r.at[b], recv_sem.at[2]).start()
+    lax.fori_loop(0, NB - 1, send_spectra, 0)
+    pltpu.make_async_copy(spec_s.at[lax.div(b, 4)], spec_r.at[b], recv_sem.at[2]).start()
 
     lines = jnp.concatenate(
         [ilc[pl.ds(k, 8, stride=8), :] for k in range(8)] + [jnp.zeros((64, 128), F32)], axis=0
@@ -330,27 +377,34 @@
             ).start()
 
     pltpu.make_async_copy(spec_r, spec_r, recv_sem.at[2]).wait()
-    start = pl.multiple_of(16 * lax.rem(b, 8), 16)
-    block = spec_r[...].astype(F32)
-    for e in range(2):
-        spec_t[e] = turn(block[:, 2 * e : 2 * e + 2, :].reshape(128, 128))
-    own_s = [spec_t[e, pl.ds(start, 16), :] for e in range(2)]
+    spec_t[...] = turn(spec_r[...].astype(F32).reshape(128, 128))
+    start = 16 * lax.rem(b, 4)
+    own_s = [spec_t[pl.ds(pl.multiple_of(64 * e + start, 16), 16), :] for e in range(2)]
     every[t] = jnp.concatenate(own_s, axis=0).astype(BF16)
-    for d in range(1, NT):
-        other = lax.rem(t + d, NT)
+    for dy, dx in FAR_FIRST:
+        other = tile_peer(t, dy, dx)
         pltpu.make_async_remote_copy(
             src_ref=every.at[t], dst_ref=every.at[t], send_sem=send_sem.at[3],
-            recv_sem=recv_sem.at[3], device_id={"band": b, "tile": other}, device_id_type=MESH,
+            recv_sem=tile_sem.at[t], device_id={"band": b, "tile": other}, device_id_type=MESH,
         ).start()
-    seven = every.at[pl.ds(0, NT - 1)]
-    pltpu.make_async_copy(seven, seven, recv_sem.at[3]).wait()
-    full = jnp.concatenate([every[q] for q in range(NT)], axis=1)
-    for s in range(16):
-        out = lax.dot_general(
-            full, leg_v[s], (((1,), (1,)), ((), ())), preferred_element_type=F32
-        )
-        alm_o[s, 0:1, :] = out[s : s + 1]
-        alm_o[s, 1:2, :] = out[16 + s : 17 + s]
+    for at, (dy, dx) in enumerate(((0, 0),) + FAR_FIRST[::-1]):
+        other = tile_peer(t, dy, dx)
+        if at:
+            pltpu.make_async_copy(every.at[other], every.at[other], tile_sem.at[other]).wait()
+        block = every[other]
+        cycles = pl.ds(pl.multiple_of(128 * other, 128), 128)
+        for s in range(16):
+            out = lax.dot_general(
+                block, leg_v[s, :, cycles], (((1,), (1,)), ((), ())), preferred_element_type=F32
+            )
+            if at == 0:
+                sums[s] = out
+            elif at < NT - 1:
+                sums[s] += out
+            else:
+                out = out + sums[s]
+                alm_o[s, 0:1, :] = out[s : s + 1]
+                alm_o[s, 1:2, :] = out[16 + s : 17 + s]
 
     pltpu.make_async_copy(cells_r, cells_r, recv_sem.at[4]).wait()
     for q in range(4):
@@ -364,7 +418,8 @@
     pltpu.make_async_copy(sent, sent, send_sem.at[1]).wait()
     sent = spec_r.at[pl.ds(0, NB - 1)]
     pltpu.make_async_copy(sent, sent, send_sem.at[2]).wait()
-    pltpu.make_async_copy(seven, seven, send_sem.at[3]).wait()
+    sent = every.at[pl.ds(0, NT - 1)]
+    pltpu.make_async_copy(sent, sent, send_sem.at[3]).wait()
     mine = owner_band == b
 
     @pl.when(mine)
@@ -381,36 +436,6 @@
     any_space = pl.BlockSpec(memory_space=pl.ANY)
     vmem = pl.BlockSpec(memory_space=pltpu.VMEM)
     first, twid, second, back, last = tables()
-    scratch = [
-        ((16, C, 2, 128), BF16),
-        ((16, 128, 1024), BF16),
-        ((8, 128), jnp.int32),
-        (first.shape, BF16),
-        (twid.shape, F32),
-        (second.shape, BF16),
-        (back.shape, BF16),
-        (last.shape, BF16),
-        ((NT, 288, 128), F32),
-        ((NT, 288, 128), BF16),
-        ((NT, 288, 128), BF16),
-        ((NB, 3, 2, 128), BF16),
-        ((NB, 3, 2, 128), BF16),
-        ((384, 128), F32),
-        ((8, 48, 128), F32),
-        ((C, 32, 128), F32),
-        ((1024, 1024), BF16),
-        ((1024, 1024), BF16),
-        ((C, 64, 128), F32),
-        ((45, 64, 128), F32),
-        ((64, 128), F32),
-        ((64, 128), F32),
-        ((64, 128), F32),
-        ((32, 128), F32),
-        ((8, 4, 128), BF16),
-        ((NB, 4, 128), BF16),
-        ((2, 128, 128), F32),
-        ((NT, 32, 128), BF16),
-    ]
     return pl.pallas_call(
         kernel,
         out_shape=(
@@ -419,14 +444,15 @@
         ),
         in_specs=[any_space] * 8,
         out_specs=(vmem, vmem),
-        scratch_shapes=[pltpu.VMEM(shape, kind) for shape, kind in scratch]
+        scratch_shapes=scratch_list()
         + [
             pltpu.SemaphoreType.DMA((11,)),
             pltpu.SemaphoreType.DMA((5,)),
             pltpu.SemaphoreType.DMA((5,)),
+            pltpu.SemaphoreType.DMA((NT,)),
         ],
         compiler_params=pltpu.CompilerParams(
-            collective_id=0, has_side_effects=True, vmem_limit_bytes=48 * 1024 * 1024
+            collective_id=0, has_side_effects=True, vmem_limit_bytes=67043328
         ),
     )(alm, legendre, order_of_slot.reshape(8, 128), first, twid, second, back, last)
 

time: 72.5 us -> 57.1 us (0.79)
  Pallas kernels: 62.4 us -> 53.5 us
  local copies, waits for them, and re-layouts: 8.94 us -> 2.7 us
    pallas_call x1, Pallas kernels: 62.4 us -> 53.5 us  [body(): pl.pallas_call(kernel, out_shape=(jax.ShapeDtypeStruct((16, 512), F32), j...]
    unnamed x18 -> x2, local copies, waits for them, and re-layouts: 8.94 us -> 2.7 us
where the time goes in v2:
time: 57.1 us; the launch traced here: 56.8 us
  Pallas kernels  53.5 us (94%)
  local copies, waits for them, and re-layouts  2.7 us (5%)
  between operations  0.64 us (1%)
    pallas_call x1, Pallas kernels, body(): pl.pallas_call(kernel, out_shape=(jax.ShapeDtypeStruct((16, 512), F32), j...  53.5 us
    unnamed x2, local copies, waits for them, and re-layouts  2.7 us

profile of v2, /device:TPU:1, one launch (start us, length us, event | category | flops | bytes accessed | tf_op | source)
XLA Modules:
  0.0 56.8 jit_solution(14575765540381142079)
XLA Ops:
  0.6 53.5 %shard_map.95 = (f32[16,512]{1,0:T(8,128)}, f32[16,2,128]{2,1,0:T(2,128)}) custom-call(bf16[16,9,2,128]{3,2,1,0:T(2,128)(2,1)} %alm_h.1, bf16[16,128,1024]{2,1,0:T(8,128)(2,1)} %leg_h.1, s32[8,128]{1,0:T(8,128)} %bitcast.1, bf16[128,64]{1,0:T(8,128)(2,1)} %constant.10.clone.first_h, f32[2,64,128]{2,1,0:T(8,128)} %constant.11.clone.twid_h, ...), custom_call_target="tpu_custom_call" | custom-call | tf_op jit(solution)/shard_map/pallas_call | solution.py:439
  54.1 1.4 %copy.12 = f32[16,512]{1,0:T(8,128)} copy(f32[16,512]{1,0:T(8,128)} %get-tuple-element.4) | data formatting | bytes 65536
  55.5 1.3 %copy.13 = f32[16,2,128]{2,1,0:T(2,128)} copy(f32[16,2,128]{2,1,0:T(2,128)} %get-tuple-element.5) | data formatting | bytes 32768

commit v3 on v2

--- a/solution.py
+++ b/solution.py
@@ -23,11 +23,8 @@
     "alm_v": ((16, C, 2, 128), BF16),
     "leg_v": ((16, 128, 1024), BF16),
     "ord_v": ((8, 128), jnp.int32),
-    "first": ((128, 64), BF16),
-    "twid": ((2, 64, 128), F32),
-    "second": ((256, 128), BF16),
-    "back": ((128, 256), BF16),
-    "last": ((128, 128), BF16),
+    "narrow": ((768, 128), BF16),
+    "twid": ((128, 128), F32),
     "stage": ((NT, 288, 128), F32),
     "parts": ((NT, 288, 128), BF16),
     "heard": ((NT, 288, 128), BF16),
@@ -80,13 +77,10 @@
     e1 = np.concatenate([-sn, cs], axis=2).reshape(16, 128)
     none = np.zeros((48, 128))
     last = np.concatenate([e0, none, e1, none], axis=0)
-    return (
-        first.astype(BF16),
-        twiddle.astype(np.float32),
-        second.astype(BF16),
-        back.astype(BF16),
-        last.astype(BF16),
-    )
+    first = np.concatenate([first, np.zeros((128, 64))], axis=1)
+    narrow = [first, second, back[:, :128], back[:, 128:], last]
+    twiddle = np.concatenate([twiddle.reshape(128, 128), np.zeros((384, 128))], axis=0)
+    return np.concatenate(narrow, axis=0).astype(BF16), twiddle.astype(np.float32)
 
 
 def pair_table():
@@ -166,6 +160,16 @@
     return (x * 16 + z) * 2 + core
 
 
+def along_z(b, dz):
+    z = lax.rem(lax.rem(lax.div(b, 2), 16) + dz, 16)
+    return (lax.div(b, 32) * 16 + z) * 2 + lax.rem(b, 2)
+
+
+def same_z(b, i):
+    x = lax.rem(lax.div(b, 32) + i // 2, 2)
+    return (x * 16 + lax.rem(lax.div(b, 2), 16)) * 2 + lax.rem(lax.rem(b, 2) + i % 2, 2)
+
+
 FAR_FIRST = ((2, 1), (1, 1), (3, 1), (2, 0), (0, 1), (1, 0), (3, 0))
 
 
@@ -178,12 +182,12 @@
 
 
 def kernel(
-    alm_h, leg_h, ord_h, first_h, twid_h, second_h, back_h, last_h,
+    alm_h, leg_h, ord_h, narrow_h, twid_h,
     map_o, alm_o,
-    alm_v, leg_v, ord_v, first, twid, second, back, last,
+    alm_v, leg_v, ord_v, narrow, twid,
     stage, parts, heard, slot_s, slot_r, turned, modes, gathered, to_order, to_slot,
     maps, smoothed, ilc, cells, cells_r, spec, spec_s, spec_r, spec_t, every, sums,
-    load_sem, send_sem, recv_sem, tile_sem,
+    load_sem, send_sem, recv_sem, tile_sem, greet_sem,
 ):
     b = lax.axis_index("band")
     t = lax.axis_index("tile")
@@ -194,8 +198,7 @@
     for at, (src, dst) in enumerate(
         [(alm_h, alm_v)]
         + [(leg_h.at[pl.ds(4 * k, 4)], leg_v.at[pl.ds(4 * k, 4)]) for k in range(4)]
-        + [(ord_h, ord_v), (first_h, first), (twid_h, twid), (second_h, second)]
-        + [(back_h, back), (last_h, last)]
+        + [(ord_h, ord_v), (narrow_h, narrow), (twid_h.at[pl.ds(0, 128)], twid)]
     ):
         copy = pltpu.make_async_copy(src, dst, load_sem.at[at])
         copy.start()
@@ -203,17 +206,15 @@
 
     bar = pltpu.get_barrier_semaphore()
 
-    def greet_band(d, _):
-        pl.semaphore_signal(
-            bar, inc=1, device_id={"band": band_peer(d, b), "tile": t}, device_id_type=MESH
-        )
-        return 0
-
-    lax.fori_loop(0, NB - 1, greet_band, 0)
-    for d in range(1, NT):
-        pl.semaphore_signal(
-            bar, inc=1, device_id={"band": b, "tile": lax.rem(t + d, NT)}, device_id_type=MESH
-        )
+    def greet(sem, others):
+        for band, tile in others:
+            pl.semaphore_signal(
+                sem, inc=1, device_id={"band": band, "tile": tile}, device_id_type=MESH
+            )
+
+    greet(bar, [(b, tile_peer(t, dy, dx)) for dy, dx in FAR_FIRST])
+    greet(bar, [(along_z(b, dz), t) for dz in (2, 14, 1, 15)])
+    greet(bar, [(same_z(b, i), t) for i in (3, 2, 1)])
 
     loads[0].wait()
     for k in range(4):
@@ -226,7 +227,8 @@
     for q in range(NT):
         parts[q] = stage[q].astype(BF16)
 
-    pl.semaphore_wait(bar, 70)
+    pl.semaphore_wait(bar, 14)
+    greet(greet_sem.at[0], [(along_z(b, dz), t) for dz in (2, 14)])
 
     for dy, dx in FAR_FIRST:
         other = tile_peer(t, dy, dx)
@@ -251,6 +253,9 @@
             to_order[s * 64 + h * 8 : s * 64 + h * 8 + 16, :] = jnp.concatenate(
                 rows, axis=0
             ).astype(BF16)
+    pl.semaphore_wait(greet_sem.at[0], 2)
+    greet(greet_sem.at[1], [(along_z(b, dz), t) for dz in (4, 12)])
+    orders = ord_v[...].astype(F32)
     tall = lax.broadcasted_iota(jnp.int32, (128, 128), 0).astype(F32)
     for h in range(8):
         row = jnp.broadcast_to(orders[h : h + 1, :], (128, 128))
@@ -259,6 +264,8 @@
                 row == tall + 128.0 * k, 1.0, 0.0
             ).astype(BF16)
 
+    pl.semaphore_wait(greet_sem.at[1], 2)
+    greet(greet_sem.at[2], [(same_z(b, i), t) for i in (3, 2, 1)])
     pltpu.make_async_copy(heard, heard, recv_sem.at[0]).wait()
     total = heard[0].astype(F32)
     for q in range(1, NT):
@@ -276,6 +283,7 @@
         ).start()
         return 0
 
+    pl.semaphore_wait(greet_sem.at[2], 3)
     lax.fori_loop(0, NB - 1, send_slots, 0)
     pltpu.make_async_copy(slot_s.at[b], slot_r.at[b], recv_sem.at[1]).start()
     pltpu.make_async_copy(slot_r, slot_r, recv_sem.at[1]).wait()
@@ -302,16 +310,16 @@
             gathered[c, 4 * k : 4 * k + 2, :] = modes[k, 2 * c : 2 * c + 2, :]
             gathered[c, 4 * k + 2 : 4 * k + 4, :] = modes[k, 24 + 2 * c : 26 + 2 * c, :]
 
-    twr, twi = twid[0], twid[1]
+    twr, twi = twid[0:64, :], twid[64:128, :]
     for c in range(C):
         data = gathered[c].astype(BF16)
         grid = jnp.dot(
-            first[...], jnp.concatenate([data, data], axis=0), preferred_element_type=F32
+            narrow[0:128, 0:64], jnp.concatenate([data, data], axis=0), preferred_element_type=F32
         )
         re, im = grid[:64], grid[64:]
         both = jnp.concatenate([re * twr - im * twi, re * twi + im * twr], axis=1)
         maps[c] = (
-            jnp.dot(both.astype(BF16), second[...], preferred_element_type=F32)
+            jnp.dot(both.astype(BF16), narrow[128:384, :], preferred_element_type=F32)
             .astype(BF16)
             .astype(F32)
         )
@@ -319,11 +327,12 @@
     window_sums(maps, smoothed)
     solve_cells(maps, smoothed, ilc)
 
-    twr, twi = twid[0], twid[1]
-    grid = jnp.dot(ilc[...].astype(BF16), back[...], preferred_element_type=F32)
-    re, im = grid[:, :128], grid[:, 128:]
+    twr, twi = twid[0:64, :], twid[64:128, :]
+    low = ilc[...].astype(BF16)
+    re = jnp.dot(low, narrow[384:512, :], preferred_element_type=F32)
+    im = jnp.dot(low, narrow[512:640, :], preferred_element_type=F32)
     both = jnp.concatenate([re * twr + im * twi, im * twr - re * twi], axis=0)
-    spec[...] = jnp.dot(last[...], both.astype(BF16), preferred_element_type=F32)
+    spec[...] = jnp.dot(narrow[640:768, :], both.astype(BF16), preferred_element_type=F32)
     flat = jnp.concatenate([spec[pl.ds(k, 16, stride=8), :] for k in range(8)], axis=1)
     placed = jnp.dot(flat.astype(BF16), to_slot[...], preferred_element_type=F32)
     half = lax.broadcasted_iota(jnp.int32, (8, 128), 1) < 64
@@ -433,28 +442,31 @@
 
 
 def body(alm, legendre, order_of_slot):
-    any_space = pl.BlockSpec(memory_space=pl.ANY)
+    hbm = pl.BlockSpec(memory_space=pltpu.HBM)
     vmem = pl.BlockSpec(memory_space=pltpu.VMEM)
-    first, twid, second, back, last = tables()
+    narrow, twid = tables()
+    operands = (alm, legendre, order_of_slot.reshape(8, 128), jnp.asarray(narrow), jnp.asarray(twid))
+    operands = [pltpu.with_memory_space_constraint(x, pltpu.HBM) for x in operands]
     return pl.pallas_call(
         kernel,
         out_shape=(
             jax.ShapeDtypeStruct((16, 512), F32),
             jax.ShapeDtypeStruct((16, 2, 128), F32),
         ),
-        in_specs=[any_space] * 8,
+        in_specs=[hbm] * 5,
         out_specs=(vmem, vmem),
         scratch_shapes=scratch_list()
         + [
-            pltpu.SemaphoreType.DMA((11,)),
+            pltpu.SemaphoreType.DMA((8,)),
             pltpu.SemaphoreType.DMA((5,)),
             pltpu.SemaphoreType.DMA((5,)),
             pltpu.SemaphoreType.DMA((NT,)),
+            pltpu.SemaphoreType.REGULAR((3,)),
         ],
         compiler_params=pltpu.CompilerParams(
-            collective_id=0, has_side_effects=True, vmem_limit_bytes=67043328
+            collective_id=0, has_side_effects=True, vmem_limit_bytes=48 * 1024 * 1024
         ),
-    )(alm, legendre, order_of_slot.reshape(8, 128), first, twid, second, back, last)
+    )(*operands)
 
 
 def solution(mesh):

time: 57.1 us -> 49.8 us (0.87)
  Pallas kernels: 53.5 us -> 47.8 us
  local copies, waits for them, and re-layouts: 2.7 us -> 1.22 us
    pallas_call x1, Pallas kernels: 53.5 us -> 47.8 us  [body(): pl.pallas_call(kernel, out_shape=(jax.ShapeDtypeStruct((16, 512), F32), j...]
    unnamed x2, local copies, waits for them, and re-layouts: 2.7 us -> 1.22 us
where the time goes in v3:
time: 49.8 us; the launch traced here: 49.7 us
  Pallas kernels  47.8 us (96%)
  local copies, waits for them, and re-layouts  1.22 us (2%)
  between operations  0.64 us (1%)
    pallas_call x1, Pallas kernels, body(): pl.pallas_call(kernel, out_shape=(jax.ShapeDtypeStruct((16, 512), F32), j...  47.8 us
    unnamed x2, local copies, waits for them, and re-layouts  1.22 us

profile of v3, /device:TPU:1, one launch (start us, length us, event | category | flops | bytes accessed | tf_op | source)
XLA Modules:
  0.0 49.7 jit_solution(6567499250046134370)
XLA Ops:
  0.6 47.8 %shard_map.68 = (f32[16,512]{1,0:T(8,128)S(1)}, f32[16,2,128]{2,1,0:T(2,128)S(1)}) custom-call(bf16[16,9,2,128]{3,2,1,0:T(2,128)(2,1)} %alm_h.1, bf16[16,128,1024]{2,1,0:T(8,128)(2,1)} %leg_h.1, s32[8,128]{1,0:T(8,128)} %bitcast.1, bf16[768,128]{1,0:T(8,128)(2,1)} %constant.4.clone.narrow_h, f32[512,128]{1,0:T(8,128)} %constant.5.clone.twid_h), custom_call_target="tpu_custom_call" | custom-call | tf_op jit(solution)/shard_map/pallas_call | solution.py:450
  48.4 0.6 %copy.9 = f32[16,512]{1,0:T(8,128)} copy(f32[16,512]{1,0:T(8,128)S(1)} %get-tuple-element.4) | data formatting | bytes 65536
  49.1 0.6 %copy.10 = f32[16,2,128]{2,1,0:T(2,128)} copy(f32[16,2,128]{2,1,0:T(2,128)S(1)} %get-tuple-element.5) | data formatting | bytes 32768

commit v4 on v3

--- a/solution.py
+++ b/solution.py
@@ -36,6 +36,7 @@
     "to_order": ((1024, 1024), BF16),
     "to_slot": ((1024, 1024), BF16),
     "maps": ((C, 64, 128), F32),
+    "ahead": ((C, 64, 128), F32),
     "smoothed": ((45, 64, 128), F32),
     "ilc": ((64, 128), F32),
     "cells": ((64, 128), F32),
@@ -107,16 +108,12 @@
             up = above[k - 1] * pltpu.roll(seg, 8 - k, 0)
             low = down if low is None else low + down
             high = up if high is None else high + up
-        total = seg + low + high
+        base = high + pltpu.roll(seg + low + high, 127, 1) + pltpu.roll(low, 126, 1)
         for i in range(8):
-            before = pltpu.roll(post[i] + high, 1, 1)
-            after = pltpu.roll(pre[i] + low, 127, 1)
-            smoothed[at, 8 * i : 8 * i + 8, :] = (before + total + after) * (
-                1.0 / (2 * HALO + 1)
-            )
-
-
-def solve_cells(maps, smoothed, out):
+            smoothed[at, 8 * i : 8 * i + 8, :] = post[i] + base + pltpu.roll(pre[i], 126, 1)
+
+
+def solve_cells(ahead, smoothed, out):
     index = {}
     for at, (a, b) in enumerate(pair_table()):
         index[a, b] = at
@@ -127,11 +124,11 @@
         trace = left[0, 0]
         for c in range(1, C):
             trace = trace + left[c, c]
-        ridge = RIDGE * (trace * (1.0 / C) + EPSILON)
+        ridge = RIDGE * (trace * (1.0 / C) + EPSILON * (2 * HALO + 1))
         for c in range(C):
             left[c, c] = left[c, c] + ridge
         ones = [jnp.ones((8, 128), F32) for _ in range(C)]
-        vals = [maps[c, rows, :] for c in range(C)]
+        vals = [ahead[c, rows, :] for c in range(C)]
         top = bottom = None
         for k in range(C):
             inverse = 1.0 / left[k, k]
@@ -148,7 +145,7 @@
         out[rows, :] = top / bottom
         return 0
 
-    lax.fori_loop(0, 8, step, 0)
+    lax.fori_loop(0, 8, step, 0, unroll=8)
 
 
 def band_peer(d, b):
@@ -186,7 +183,7 @@
     map_o, alm_o,
     alm_v, leg_v, ord_v, narrow, twid,
     stage, parts, heard, slot_s, slot_r, turned, modes, gathered, to_order, to_slot,
-    maps, smoothed, ilc, cells, cells_r, spec, spec_s, spec_r, spec_t, every, sums,
+    maps, ahead, smoothed, ilc, cells, cells_r, spec, spec_s, spec_r, spec_t, every, sums,
     load_sem, send_sem, recv_sem, tile_sem, greet_sem,
 ):
     b = lax.axis_index("band")
@@ -318,14 +315,14 @@
         )
         re, im = grid[:64], grid[64:]
         both = jnp.concatenate([re * twr - im * twi, re * twi + im * twr], axis=1)
-        maps[c] = (
-            jnp.dot(both.astype(BF16), narrow[128:384, :], preferred_element_type=F32)
-            .astype(BF16)
-            .astype(F32)
-        )
+        found = jnp.dot(both.astype(BF16), narrow[128:384, :], preferred_element_type=F32)
+        found = found.astype(BF16).astype(F32)
+        maps[c] = found
+        ahead[c] = pltpu.roll(found, 127, 1)
 
     window_sums(maps, smoothed)
-    solve_cells(maps, smoothed, ilc)
+    solve_cells(ahead, smoothed, ilc)
+    ilc[...] = pltpu.roll(ilc[...], 1, 1)
 
     twr, twi = twid[0:64, :], twid[64:128, :]
     low = ilc[...].astype(BF16)
@@ -447,7 +444,7 @@
     narrow, twid = tables()
     operands = (alm, legendre, order_of_slot.reshape(8, 128), jnp.asarray(narrow), jnp.asarray(twid))
     operands = [pltpu.with_memory_space_constraint(x, pltpu.HBM) for x in operands]
-    return pl.pallas_call(
+    found = pl.pallas_call(
         kernel,
         out_shape=(
             jax.ShapeDtypeStruct((16, 512), F32),
@@ -467,6 +464,27 @@
             collective_id=0, has_side_effects=True, vmem_limit_bytes=48 * 1024 * 1024
         ),
     )(*operands)
+    return pl.pallas_call(
+        hand_on,
+        out_shape=(
+            jax.ShapeDtypeStruct((16, 512), F32),
+            jax.ShapeDtypeStruct((16, 2, 128), F32),
+        ),
+        in_specs=[vmem] * 2,
+        out_specs=(pl.BlockSpec(memory_space=pltpu.HBM),) * 2,
+        scratch_shapes=[pltpu.SemaphoreType.DMA((2,))],
+    )(*[pltpu.with_memory_space_constraint(x, pltpu.VMEM) for x in found])
+
+
+def hand_on(map_i, alm_i, map_o, alm_o, sem):
+    copies = [
+        pltpu.make_async_copy(map_i, map_o, sem.at[0]),
+        pltpu.make_async_copy(alm_i, alm_o, sem.at[1]),
+    ]
+    for copy in copies:
+        copy.start()
+    for copy in copies:
+        copy.wait()
 
 
 def solution(mesh):

time: 49.8 us -> 48.5 us (0.974)
  local copies, waits for them, and re-layouts: 1.22 us -> 0 us
    unnamed x2 -> x0, local copies, waits for them, and re-layouts: 1.22 us -> none
    pallas_call x1, Pallas kernels: 47.8 us -> 47.1 us  [body(): pl.pallas_call(kernel, out_shape=(jax.ShapeDtypeStruct((16, 512), F32), j...]
    pallas_call x0 -> x1, Pallas kernels: none -> 0.64 us  [body(): pl.pallas_call(hand_on, out_shape=(jax.ShapeDtypeStruct((16, 512), F32),...]
where the time goes in v4:
time: 48.5 us; the launch traced here: 48.4 us
  Pallas kernels  47.8 us (99%)
  between operations  0.64 us (1%)
    pallas_call x1, Pallas kernels, body(): pl.pallas_call(kernel, out_shape=(jax.ShapeDtypeStruct((16, 512), F32), j...  47.1 us

profile of v4, /device:TPU:1, one launch (start us, length us, event | category | flops | bytes accessed | tf_op | source)
XLA Modules:
  0.0 48.4 jit_solution(2224475032642925673)
XLA Ops:
  0.6 47.1 %shard_map.68 = (f32[16,512]{1,0:T(8,128)S(1)}, f32[16,2,128]{2,1,0:T(2,128)S(1)}) custom-call(bf16[16,9,2,128]{3,2,1,0:T(2,128)(2,1)} %alm_h.1, bf16[16,128,1024]{2,1,0:T(8,128)(2,1)} %leg_h.1, s32[8,128]{1,0:T(8,128)} %bitcast.1, bf16[768,128]{1,0:T(8,128)(2,1)} %constant.4.clone.narrow_h, f32[512,128]{1,0:T(8,128)} %constant.5.clone.twid_h), custom_call_target="tpu_custom_call" | custom-call | tf_op jit(solution)/shard_map/pallas_call | solution.py:447
  47.8 0.6 %shard_map.69 = (f32[16,512]{1,0:T(8,128)}, f32[16,2,128]{2,1,0:T(2,128)}) custom-call(f32[16,512]{1,0:T(8,128)S(1)} %get-tuple-element.4.map_i, f32[16,2,128]{2,1,0:T(2,128)S(1)} %get-tuple-element.5.alm_i), custom_call_target="tpu_custom_call" | custom-call | tf_op jit(solution)/shard_map/pallas_call | solution.py:467

commit v5 on v4

--- a/solution.py
+++ b/solution.py
@@ -31,6 +31,7 @@
     "slot_s": ((NB, 3, 2, 128), BF16),
     "slot_r": ((NB, 3, 2, 128), BF16),
     "turned": ((384, 128), F32),
+    "mixed": ((3, 128, 128), F32),
     "modes": ((8, 48, 128), F32),
     "gathered": ((C, 32, 128), F32),
     "to_order": ((1024, 1024), BF16),
@@ -182,7 +183,7 @@
     alm_h, leg_h, ord_h, narrow_h, twid_h,
     map_o, alm_o,
     alm_v, leg_v, ord_v, narrow, twid,
-    stage, parts, heard, slot_s, slot_r, turned, modes, gathered, to_order, to_slot,
+    stage, parts, heard, slot_s, slot_r, turned, mixed, modes, gathered, to_order, to_slot,
     maps, ahead, smoothed, ilc, cells, cells_r, spec, spec_s, spec_r, spec_t, every, sums,
     load_sem, send_sem, recv_sem, tile_sem, greet_sem,
 ):
@@ -286,9 +287,10 @@
     pltpu.make_async_copy(slot_r, slot_r, recv_sem.at[1]).wait()
 
     for k in range(3):
-        block = slot_r[:, k].astype(F32)
-        block = jnp.concatenate([block[:, 0, :], block[:, 1, :]], axis=0)
-        turned[128 * k : 128 * k + 128, :] = turn(block)
+        mixed[k] = slot_r[:, k].astype(F32).reshape(128, 128)
+    for k in range(3):
+        block = [mixed[k, pl.ds(j, 64, stride=2), :] for j in range(2)]
+        turned[128 * k : 128 * k + 128, :] = turn(jnp.concatenate(block, axis=0))
     lane24 = lax.broadcasted_iota(jnp.int32, (24, 128), 1)
     pieces = []
     for p in range(8):
@@ -308,6 +310,7 @@
             gathered[c, 4 * k + 2 : 4 * k + 4, :] = modes[k, 24 + 2 * c : 26 + 2 * c, :]
 
     twr, twi = twid[0:64, :], twid[64:128, :]
+    rows = []
     for c in range(C):
         data = gathered[c].astype(BF16)
         grid = jnp.dot(
@@ -315,8 +318,12 @@
         )
         re, im = grid[:64], grid[64:]
         both = jnp.concatenate([re * twr - im * twi, re * twi + im * twr], axis=1)
-        found = jnp.dot(both.astype(BF16), narrow[128:384, :], preferred_element_type=F32)
-        found = found.astype(BF16).astype(F32)
+        rows.append(both.astype(BF16))
+    whole = jnp.dot(
+        jnp.concatenate(rows, axis=0), narrow[128:384, :], preferred_element_type=F32
+    )
+    for c in range(C):
+        found = whole[64 * c : 64 * c + 64].astype(BF16).astype(F32)
         maps[c] = found
         ahead[c] = pltpu.roll(found, 127, 1)
 
@@ -395,6 +402,12 @@
         ).start()
     for at, (dy, dx) in enumerate(((0, 0),) + FAR_FIRST[::-1]):
         other = tile_peer(t, dy, dx)
+        if at == NT - 1:
+            pltpu.make_async_copy(cells_r, cells_r, recv_sem.at[4]).wait()
+            for q in range(4):
+                for j in range(2):
+                    ilc[pl.ds(16 * q + j, 8, stride=2), :] = cells_r[pl.ds(2 * q + j, 8, stride=8), :]
+                map_o[:, 128 * q : 128 * q + 128] = ilc[16 * q : 16 * q + 16, :]
         if at:
             pltpu.make_async_copy(every.at[other], every.at[other], tile_sem.at[other]).wait()
         block = every[other]
@@ -411,12 +424,6 @@
                 out = out + sums[s]
                 alm_o[s, 0:1, :] = out[s : s + 1]
                 alm_o[s, 1:2, :] = out[16 + s : 17 + s]
-
-    pltpu.make_async_copy(cells_r, cells_r, recv_sem.at[4]).wait()
-    for q in range(4):
-        for j in range(2):
-            ilc[pl.ds(16 * q + j, 8, stride=2), :] = cells_r[pl.ds(2 * q + j, 8, stride=8), :]
-        map_o[:, 128 * q : 128 * q + 128] = ilc[16 * q : 16 * q + 16, :]
 
     sent = parts.at[pl.ds(0, NT - 1)]
     pltpu.make_async_copy(sent, sent, send_sem.at[0]).wait()

time: 48.5 us -> 48.8 us (level)
  no operation moved by 1% of the time
where the time goes in v5:
time: 48.8 us; the launch traced here: 48.7 us
  Pallas kernels  48.1 us (99%)
  between operations  0.64 us (1%)
    pallas_call x1, Pallas kernels, body(): pl.pallas_call(kernel, out_shape=(jax.ShapeDtypeStruct((16, 512), F32), j...  47.4 us

profile of v5, /device:TPU:1, one launch (start us, length us, event | category | flops | bytes accessed | tf_op | source)
XLA Modules:
  0.0 48.7 jit_solution(13725517860132907529)
XLA Ops:
  0.6 47.4 %shard_map.68 = (f32[16,512]{1,0:T(8,128)S(1)}, f32[16,2,128]{2,1,0:T(2,128)S(1)}) custom-call(bf16[16,9,2,128]{3,2,1,0:T(2,128)(2,1)} %alm_h.1, bf16[16,128,1024]{2,1,0:T(8,128)(2,1)} %leg_h.1, s32[8,128]{1,0:T(8,128)} %bitcast.1, bf16[768,128]{1,0:T(8,128)(2,1)} %constant.4.clone.narrow_h, f32[512,128]{1,0:T(8,128)} %constant.5.clone.twid_h), custom_call_target="tpu_custom_call" | custom-call | tf_op jit(solution)/shard_map/pallas_call | solution.py:454
  48.1 0.6 %shard_map.69 = (f32[16,512]{1,0:T(8,128)}, f32[16,2,128]{2,1,0:T(2,128)}) custom-call(f32[16,512]{1,0:T(8,128)S(1)} %get-tuple-element.4.map_i, f32[16,2,128]{2,1,0:T(2,128)S(1)} %get-tuple-element.5.alm_i), custom_call_target="tpu_custom_call" | custom-call | tf_op jit(solution)/shard_map/pallas_call | solution.py:474
